TPU v7x, 32 devices: a whole 2x2x4 slice. The times are simulated.
32 devices in a mesh: grp: 2 (over y), sec: 4 (over z), blk: 2 (over x), op: 2 (over core).
Axes of the slice: x: 2, y: 2, z: 4, core: 2. Of those that a mesh axis runs over, the one named last changes fastest.
Arguments:
- ground_state: bfloat16 [48, 512, 512], P(('grp', 'sec'), 'blk'), parts along dimension 0, may hold values from -6 to 6
- op_matrices: bfloat16 [16, 512, 512], P(('grp', 'op')), parts along dimension 0, may hold values from -0.25 to 0.25
- shift_map: int32 [16, 24], P('grp'), parts along dimension 0, may hold values from 0 to 23, as said below
- new_slot: int32 [48], P('grp'), parts along dimension 0, may hold values from 0 to 23, as said below
- env_ground: bfloat16 [48, 512, 512], P(('grp', 'sec'), 'blk'), parts along dimension 0, may hold values from -0.25 to 0.25
- env_src: int32 [48, 3], P('grp'), parts along dimension 0, may hold values from 0 to 23, as said below
- env_coef: float32 [48, 3], P('grp'), parts along dimension 0, may hold values from 0.3 to 1
Outputs:
- grown_env: bfloat16 [16, 24, 512, 512], P(('grp', 'op'), 'sec', 'blk'), parts along dimension 0
There are 2 independent parts, one for each index of `grp`. A program takes and returns all parts, laid end to end along the dimension named above; each array names one. Nothing has to cross between parts.
Inputs may be any that keep to these rules, and one draw needn't show every extreme that they name: Each row o maps the 24 ground sectors one to one onto the N+1 sectors. Within each group of 4 consecutive operators, among the pairs (o, s) with one value of s // 6, at most 7 have new_slot[shift_map[o, s]] // 6 equal to one value, and 7 is reached for every value of s // 6. A permutation: N+1 sector t is stored at slot new_slot[t]. For the N+1 sectors t with one value of new_slot[t] // 6, at most 6 of the entries env_src[t, k] have one value of env_src[t, k] // 6, and 6 is reached for every value of new_slot[t] // 6.
All inputs are finite; a program needn't handle non-finite values.
Results may differ from a plain program's by a relative error of at most 0.0057.
Values may be sent and summed in bfloat16 or wider, within the bound.
No kernel may reach another device: no remote copies, remote signals or barrier semaphores. Data moves between devices by JAX's collectives and lax.ppermute only.
A program may use at most 64 MiB of HBM per device.

v0:
```python
import jax
import jax.numpy as jnp
from jax import lax
from jax.sharding import PartitionSpec as P


def pair_ranks(pair_key):
    counter = jnp.arange(pair_key.shape[0])
    same_pair = pair_key[:, None] == pair_key[None, :]
    earlier = counter[None, :] < counter[:, None]
    return jnp.sum((same_pair & earlier).astype(jnp.int32), axis=1)


def local(ground_state, op_matrices, shift_map, new_slot, env_ground, env_src, env_coef):
    owner_count = lax.axis_size("sec")
    owner = lax.axis_index("sec")
    op_group = lax.axis_index("op")
    sec_dev, row_count, columns = ground_state.shape
    ops_dev = op_matrices.shape[0]
    env_terms = env_src.shape[1]
    sectors = sec_dev * owner_count
    capacity = (sec_dev * ops_dev + owner_count - 1) // owner_count + 1
    env_capacity = (sec_dev * env_terms + owner_count - 1) // owner_count + 1
    dest_all = jnp.take(new_slot, shift_map)
    dest_grp = lax.dynamic_slice_in_dim(dest_all, op_group * ops_dev, ops_dev, 0)
    source_of = jnp.argsort(dest_grp, axis=1)
    sources = lax.dynamic_slice_in_dim(source_of, owner * sec_dev, sec_dev, 1)
    products = jnp.einsum(
        "srd,ode->sore", ground_state, op_matrices, preferred_element_type=jnp.float32
    ).astype(jnp.bfloat16)
    entry_ids = jnp.arange(sectors * ops_dev)
    entry_sector = entry_ids // ops_dev
    entry_dest = dest_grp[entry_ids % ops_dev, entry_sector]
    ranking = pair_ranks(entry_sector // sec_dev * owner_count + entry_dest // sec_dev)
    positions = lax.dynamic_slice_in_dim(
        entry_dest // sec_dev * capacity + ranking, owner * sec_dev * ops_dev, sec_dev * ops_dev
    )
    outgoing = jnp.zeros((owner_count * capacity, row_count, columns), jnp.bfloat16)
    outgoing = outgoing.at[positions].set(products.reshape(sec_dev * ops_dev, row_count, columns))
    incoming = lax.all_to_all(outgoing, "sec", split_axis=0, concat_axis=0, tiled=True)
    wanted = sources * ops_dev + jnp.arange(ops_dev)[:, None]
    locate = sources // sec_dev * capacity + ranking[wanted]
    arrived = incoming[locate]
    sector_at = jnp.argsort(new_slot)
    my_sectors = lax.dynamic_slice_in_dim(sector_at, owner * sec_dev, sec_dev)
    my_coef = env_coef[my_sectors]
    flat_src = env_src[sector_at].reshape(-1)
    entry_slot = jnp.arange(sectors * env_terms) // env_terms
    ranking_env = pair_ranks(flat_src // sec_dev * owner_count + entry_slot // sec_dev)
    placing = entry_slot // sec_dev * env_capacity + ranking_env
    is_mine = flat_src // sec_dev == owner
    slot_ids = jnp.arange(owner_count * env_capacity)
    hit_table = ((placing[None, :] == slot_ids[:, None]) & is_mine[None, :]).astype(jnp.float32)
    local_table = ((flat_src - owner * sec_dev)[:, None] == jnp.arange(sec_dev)[None, :]).astype(
        jnp.float32
    )
    selector = jnp.dot(hit_table, local_table, precision=lax.Precision.HIGHEST).astype(jnp.bfloat16)
    outgoing_env = jnp.einsum(
        "pi,ird->prd", selector, env_ground, preferred_element_type=jnp.float32
    ).astype(jnp.bfloat16)
    incoming_env = lax.all_to_all(outgoing_env, "sec", split_axis=0, concat_axis=0, tiled=True)
    mine_entries = (owner * sec_dev + jnp.arange(sec_dev))[:, None] * env_terms + jnp.arange(
        env_terms
    )[None, :]
    locate_env = flat_src[mine_entries] // sec_dev * env_capacity + ranking_env[mine_entries]
    blocks = incoming_env[locate_env].astype(jnp.float32)
    mixed = jnp.sum(my_coef[:, :, None, None] * blocks, axis=1)
    env_rounded = mixed.astype(jnp.bfloat16)
    grown_env = jnp.einsum(
        "olrd,lde->olre",
        arrived,
        lax.all_gather(env_rounded, "blk", axis=1, tiled=True),
        preferred_element_type=jnp.float32,
    )
    return grown_env.astype(jnp.bfloat16)


def solution(mesh):
    return jax.shard_map(
        local,
        mesh=mesh,
        in_specs=(
            P(("grp", "sec"), "blk", None),
            P(("grp", "op"), None, None),
            P("grp", None),
            P("grp"),
            P(("grp", "sec"), "blk", None),
            P("grp", None),
            P("grp", None),
        ),
        out_specs=P(("grp", "op"), "sec", "blk", None),
        check_vma=False,
    )
```

profile of v0, /device:TPU:0, one launch (start us, length us, event | category | flops | bytes accessed | tf_op | source)
XLA Modules:
  0.0 368.2 jit_solution(6414172959295741181)
XLA Ops:
  6.6 0.8 compare_select_fusion.2
  7.5 1.9 gather_fusion.5
  9.5 0.7 and_select_fusion
  10.2 1.5 gather_fusion.6
  11.7 0.2 convert_reduce_fusion
  11.9 2.3 sort.34
  14.2 0.8 copy.39
  15.0 0.6 gather_fusion.1
  15.7 0.2 convert_reduce_fusion.1
  15.9 0.2 fusion.9
  16.2 3.3 convolution_convert_fusion
  19.5 4.9 %copy.41 = bf16[24,256,512]{2,1,0:T(8,128)(2,1)} copy(bf16[24,256,512]{2,0,1:T(8,128)(2,1)S(1)} %convolution_convert_fusion) | data formatting | bytes 12582912 | tf_op jit(solution)/shard_map/convert_element_type | solution.py:60
  24.3 6.3 %all-to-all-start = ((bf16[24,256,512]{2,1,0:T(8,128)(2,1)}), bf16[24,256,512]{2,1,0:T(8,128)(2,1)}, u32[]{:S(2)}, u32[]{:S(2)}) async-start(bf16[24,256,512]{2,1,0:T(8,128)(2,1)} %copy.41), calls=%async_computation | async-start | bytes 12582912 | tf_op jit(solution)/shard_map/all_to_all | solution.py:61
  30.7 6.8 %convert_bitcast_fusion.1 = bf16[6,4,256,512]{2,3,0,1:T(8,128)(2,1)} fusion(bf16[4,512,512]{2,1,0:T(8,128)(2,1)S(1)} %copy-done, bf16[6,256,512]{2,1,0:T(8,128)(2,1)} %param.7), kind=kOutput, calls=%fused_computation.15 | convolution fusion | flops 3224371200 | bytes 9961472 | tf_op jit(solution)/shard_map/srd,ode->sore/dot_general | solution.py:28
  37.5 8.7 %copy.44 = bf16[6,4,256,512]{3,2,1,0:T(8,128)(2,1)} copy(bf16[6,4,256,512]{2,3,0,1:T(8,128)(2,1)} %convert_bitcast_fusion.1) | data formatting | bytes 12582912 | tf_op jit(solution)/shard_map/convert_element_type | solution.py:30
  46.1 3.8 %broadcast_in_dim.22 = bf16[28,256,512]{2,1,0:T(8,128)(2,1)} broadcast(bf16[]{:T(256)} %constant.123.clone.1), dimensions={} | broadcast | bytes 7340034 | tf_op jit(solution)/shard_map/broadcast_in_dim | solution.py:38
  49.9 16.2 %scatter_fusion = bf16[28,256,512]{2,1,0:T(8,128)(2,1)} fusion(bf16[28,256,512]{2,1,0:T(8,128)(2,1)} %broadcast_in_dim.22, s32[24]{0:T(128)S(1)} %get-tuple-element.13, bf16[24,256,512]{2,1,0:T(8,128)(2,1)} %bitcast.30), kind=kCustom, calls=%fused_computation.9 | custom fusion | bytes 18874464 | tf_op jit(solution)/shard_map/scatter | solution.py:39
  66.1 103.3 %all-to-all-done = bf16[24,256,512]{2,1,0:T(8,128)(2,1)} async-done(((bf16[24,256,512]{2,1,0:T(8,128)(2,1)}), bf16[24,256,512]{2,1,0:T(8,128)(2,1)}, u32[]{:S(2)}, u32[]{:S(2)}) %all-to-all-start) | async-done | bytes 6291488 | tf_op jit(solution)/shard_map/all_to_all | solution.py:61
  169.4 5.4 %all-to-all-start.1 = ((bf16[28,256,512]{2,1,0:T(8,128)(2,1)}), bf16[28,256,512]{2,1,0:T(8,128)(2,1)}, u32[]{:S(2)}, u32[]{:S(2)}) async-start(bf16[28,256,512]{2,1,0:T(8,128)(2,1)} %scatter_fusion), calls=%async_computation.1 | async-start | bytes 14680064 | tf_op jit(solution)/shard_map/all_to_all | solution.py:40
  174.8 0.2 all-gather.2.cloned.1.call-start
  175.3 0.7 gather_fusion.3
  176.0 0.7 gather_fusion.2
  177.2 0.6 gather_fusion
  177.8 6.8 %gather_fusion.4 = bf16[18,256,512]{2,1,0:T(8,128)(2,1)} fusion(bf16[24,256,512]{2,1,0:T(8,128)(2,1)} %all-to-all-done, s32[1024]{0:T(1024)S(1)} %pad_clamp_fusion.3), kind=kCustom, calls=%fused_computation.4 | custom fusion | bytes 9437256 | tf_op jit(solution)/shard_map/gather | solution.py:66
  184.5 3.4 fusion
  187.9 1.6 copy.42
  189.6 0.8 sort.35
  190.6 0.7 gather_fusion.7
  191.7 143.5 %all-to-all-done.1 = bf16[28,256,512]{2,1,0:T(8,128)(2,1)} async-done(((bf16[28,256,512]{2,1,0:T(8,128)(2,1)}), bf16[28,256,512]{2,1,0:T(8,128)(2,1)}, u32[]{:S(2)}, u32[]{:S(2)}) %all-to-all-start.1) | async-done | bytes 7340064 | tf_op jit(solution)/shard_map/all_to_all | solution.py:40
  335.2 7.6 %gather_fusion.8 = bf16[24,256,512]{2,1,0:T(8,128)(2,1)} fusion(bf16[28,256,512]{2,1,0:T(8,128)(2,1)} %all-to-all-done.1, s32[1024]{0:T(1024)S(1)} %pad_clamp_fusion), kind=kCustom, calls=%fused_computation.8 | custom fusion | bytes 12583008 | tf_op jit(solution)/shard_map/gather | solution.py:43
  342.7 10.0 %convert_bitcast_fusion = bf16[4,6,256,512]{2,3,0,1:T(8,128)(2,1)} fusion(bf16[4,6,256,512]{3,2,1,0:T(8,128)(2,1)} %bitcast.32, bf16[6,512,512]{1,2,0:T(8,128)(2,1)} %all-gather.2.cloned.1.call-done), kind=kOutput, calls=%fused_computation.14 | convolution fusion | flops 3224371200 | bytes 15728640 | tf_op jit(solution)/shard_map/olrd,lde->olre/dot_general | solution.py:69
  352.7 8.6 %copy.50 = bf16[4,6,256,512]{3,2,1,0:T(8,128)(2,1)} copy(bf16[4,6,256,512]{2,3,0,1:T(8,128)(2,1)} %convert_bitcast_fusion) | data formatting | bytes 12582912 | tf_op jit(solution)/shard_map/convert_element_type | solution.py:75
  (50 shorter events, 1.9 us)
Async XLA Ops:
  6.5 24.1 %copy-start = (bf16[4,512,512]{2,1,0:T(8,128)(2,1)S(1)}, bf16[4,512,512]{2,1,0:T(8,128)(2,1)}, u32[]{:S(2)}) copy-start(bf16[4,512,512]{2,1,0:T(8,128)(2,1)} %param.8) | copy-start | bytes 6291460
  24.3 145.1 %all-to-all-start = ((bf16[24,256,512]{2,1,0:T(8,128)(2,1)}), bf16[24,256,512]{2,1,0:T(8,128)(2,1)}, u32[]{:S(2)}, u32[]{:S(2)}) async-start(bf16[24,256,512]{2,1,0:T(8,128)(2,1)} %copy.41), calls=%async_computation | async-start | bytes 12582912 | tf_op jit(solution)/shard_map/all_to_all | solution.py:61
  169.4 165.7 %all-to-all-start.1 = ((bf16[28,256,512]{2,1,0:T(8,128)(2,1)}), bf16[28,256,512]{2,1,0:T(8,128)(2,1)}, u32[]{:S(2)}, u32[]{:S(2)}) async-start(bf16[28,256,512]{2,1,0:T(8,128)(2,1)} %scatter_fusion), calls=%async_computation.1 | async-start | bytes 14680064 | tf_op jit(solution)/shard_map/all_to_all | solution.py:40
  174.8 2.2 copy-start.2
  174.8 167.9 %all-gather.2.cloned.1.call-start = ((), (), s32[]{:S(2)}) async-start(), calls=%async_computation.2 | async-start | bytes 4718592 | tf_op jit(solution)/shard_map/all_gather | solution.py:72
  342.7 18.7 %copy-start.1 = (bf16[4,512,512]{2,1,0:T(8,128)(2,1)S(1)}, bf16[4,512,512]{2,1,0:T(8,128)(2,1)}, u32[]{:S(2)}) copy-start(bf16[4,512,512]{2,1,0:T(8,128)(2,1)} %param.8) | copy-start | bytes 6291460
Sparse Core Ops, SparseCore 0:
  189.6 46.1 all-gather.1
where the time goes:
time: 369 us; the launch traced here: 368 us
  waiting for transfers between devices  247 us (67%)
  local copies, waits for them, and re-layouts  66.8 us (18%)
  matrix products  20.3 us (6%)
  between operations  13.5 us (4%)
  starting transfers between devices  12 us (3%)
  other arithmetic  8.77 us (2%)
    all_to_all x1, waiting for transfers between devices, local(): lax.all_to_all(outgoing, 'sec', split_axis=0, concat_axis=0, tiled=True)  143 us
    all_to_all x1, waiting for transfers between devices, local(): lax.all_to_all(outgoing_env, 'sec', split_axis=0, concat_axis=0, tiled=True)  103 us
    scatter x1, local copies, waits for them, and re-layouts, local(): outgoing.at[positions]  16.2 us
    dot_general x1, matrix products, local(): jnp.einsum('olrd,lde->olre', arrived, lax.all_gather(env_rounded, 'blk',...  10 us
    convert_element_type x1, local copies, waits for them, and re-layouts, local(): products = jnp.einsum('srd,ode->sore', ground_state, op_matrices, preferr...  8.66 us
    convert_element_type x1, local copies, waits for them, and re-layouts, local(): return grown_env.astype(jnp.bfloat16)  8.64 us
    gather x1, local copies, waits for them, and re-layouts, local(): arrived = incoming[locate]  7.57 us
  transfers between devices with their start and end apart: 3, of which 2 were waited for; matrix products, arithmetic and copies ran while one was open for 16% of the time, Pallas kernels for 0%

commit v1 on v0

--- a/solution.py
+++ b/solution.py
@@ -2,6 +2,18 @@
 import jax.numpy as jnp
 from jax import lax
 from jax.sharding import PartitionSpec as P
+
+
+def split_up(x, dim, size):
+    shape = x.shape
+    tiles = x.reshape(*shape[:dim], size, shape[dim] // size, *shape[dim + 1 :])
+    return jnp.moveaxis(tiles, dim, 0)
+
+
+def joined_along(blocks, dim):
+    shape = list(blocks.shape[1:])
+    shape[dim] *= blocks.shape[0]
+    return jnp.moveaxis(blocks, 0, dim).reshape(shape)
 
 
 def pair_ranks(pair_key):
@@ -58,7 +70,14 @@
     outgoing_env = jnp.einsum(
         "pi,ird->prd", selector, env_ground, preferred_element_type=jnp.float32
     ).astype(jnp.bfloat16)
-    incoming_env = lax.all_to_all(outgoing_env, "sec", split_axis=0, concat_axis=0, tiled=True)
+    peers, index = (lax.axis_size("sec"), lax.axis_index("sec"))
+    tiles = split_up(outgoing_env, 0, peers)
+    gathered = [tiles[index]]
+    for step in range(1, peers):
+        sent = tiles[(index + step) % peers]
+        gathered.append(lax.ppermute(sent, "sec", [(i, (i + step) % peers) for i in range(peers)]))
+    tiles = jnp.stack(gathered)[(index - jnp.arange(peers)) % peers]
+    incoming_env = joined_along(tiles, 0)
     mine_entries = (owner * sec_dev + jnp.arange(sec_dev))[:, None] * env_terms + jnp.arange(
         env_terms
     )[None, :]

time: 369 us -> 446 us (1.21)
  waiting for transfers between devices: 247 us -> 308 us
  local copies, waits for them, and re-layouts: 66.8 us -> 78.2 us
  other arithmetic: 8.77 us -> 14.6 us
    ppermute x0 -> x3, waiting for transfers between devices: none -> 275 us  [local(): lax.ppermute(sent, 'sec', [(i, (i + step) % peers) for i in range(peers)])]
    all_to_all x1, waiting for transfers between devices: 143 us -> 0.01 us  [local(): lax.all_to_all(outgoing, 'sec', split_axis=0, concat_axis=0, tiled=True)]
    all_to_all x1 -> x0, waiting for transfers between devices: 103 us -> none  [local(): lax.all_to_all(outgoing_env, 'sec', split_axis=0, concat_axis=0, tiled=True)]
    all_gather x1, waiting for transfers between devices: 0.01 us -> 33.2 us  [local(): lax.all_gather(env_rounded, 'blk', axis=1, tiled=True)]
    all_to_all x1 -> x0, starting transfers between devices: 6.32 us -> none  [local(): lax.all_to_all(outgoing_env, 'sec', split_axis=0, concat_axis=0, tiled=True)]
    gather x0 -> x1, local copies, waits for them, and re-layouts: none -> 6.3 us  [local(): tiles = jnp.stack(gathered)[(index - jnp.arange(peers)) % peers]]
    another operation x0 -> x1, other arithmetic: none -> 5.78 us  [local(): tiles = jnp.stack(gathered)[(index - jnp.arange(peers)) % peers]]
    ppermute x0 -> x3, starting transfers between devices: none -> 5.17 us  [local(): lax.ppermute(sent, 'sec', [(i, (i + step) % peers) for i in range(peers)])]
  transfers between devices with their start and end apart: 3 -> 5, of which waited for: 2 -> 3; matrix products, arithmetic and copies ran while one was open for 16% -> 11% of each run, Pallas kernels for 0% -> 0%
where the time goes in v1:
time: 446 us; the launch traced here: 445 us
  waiting for transfers between devices  308 us (69%)
  local copies, waits for them, and re-layouts  78.2 us (18%)
  matrix products  19.2 us (4%)
  other arithmetic  14.6 us (3%)
  between operations  13.5 us (3%)
  starting transfers between devices  11.7 us (3%)
    ppermute x3, waiting for transfers between devices, local(): lax.ppermute(sent, 'sec', [(i, (i + step) % peers) for i in range(peers)])  275 us
    all_gather x1, waiting for transfers between devices, local(): lax.all_gather(env_rounded, 'blk', axis=1, tiled=True)  33.2 us
    scatter x1, local copies, waits for them, and re-layouts, local(): outgoing.at[positions]  16.2 us
    dot_general x1, matrix products, local(): jnp.einsum('olrd,lde->olre', arrived, lax.all_gather(env_rounded, 'blk',...  10 us
  transfers between devices with their start and end apart: 5, of which 3 were waited for; matrix products, arithmetic and copies ran while one was open for 11% of the time, Pallas kernels for 0%

profile of v1, /device:TPU:0, one launch (start us, length us, event | category | flops | bytes accessed | tf_op | source)
XLA Modules:
  0.0 445.1 jit_solution(14796988350252759221)
XLA Ops:
  6.6 0.8 compare_select_fusion.2
  7.5 1.9 gather_fusion.6
  9.5 0.7 and_select_fusion
  10.2 1.5 gather_fusion.7
  11.9 2.3 sort.34
  14.2 6.8 %convert_bitcast_fusion.1 = bf16[6,4,256,512]{2,3,0,1:T(8,128)(2,1)} fusion(bf16[4,512,512]{2,1,0:T(8,128)(2,1)S(1)} %copy-done, bf16[6,256,512]{2,1,0:T(8,128)(2,1)} %param.7), kind=kOutput, calls=%fused_computation.17 | convolution fusion | flops 3224371200 | bytes 9961472 | tf_op jit(solution)/shard_map/srd,ode->sore/dot_general | solution.py:40
  21.0 8.7 %copy.44 = bf16[6,4,256,512]{3,2,1,0:T(8,128)(2,1)} copy(bf16[6,4,256,512]{2,3,0,1:T(8,128)(2,1)} %convert_bitcast_fusion.1) | data formatting | bytes 12582912 | tf_op jit(solution)/shard_map/convert_element_type | solution.py:42
  29.7 3.8 broadcast_in_dim.22
  33.6 16.2 %scatter_fusion = bf16[28,256,512]{2,1,0:T(8,128)(2,1)} fusion(bf16[28,256,512]{2,1,0:T(8,128)(2,1)} %broadcast_in_dim.22, s32[24]{0:T(128)S(1)} %get-tuple-element.17, bf16[24,256,512]{2,1,0:T(8,128)(2,1)} %bitcast.44), kind=kCustom, calls=%fused_computation.10 | custom fusion | bytes 18874464 | tf_op jit(solution)/shard_map/scatter | solution.py:51
  49.8 6.5 %all-to-all-start = ((bf16[28,256,512]{2,1,0:T(8,128)(2,1)}), bf16[28,256,512]{2,1,0:T(8,128)(2,1)}, u32[]{:S(2)}, u32[]{:S(2)}) async-start(bf16[28,256,512]{2,1,0:T(8,128)(2,1)} %scatter_fusion), calls=%async_computation | async-start | bytes 14680064 | tf_op jit(solution)/shard_map/all_to_all | solution.py:52
  56.4 0.6 gather_fusion.1
  57.5 2.1 convolution_convert_fusion
  59.7 5.0 %copy.41 = bf16[24,256,512]{2,1,0:T(8,128)(2,1)} copy(bf16[24,256,512]{2,0,1:T(8,128)(2,1)S(1)} %convolution_convert_fusion) | data formatting | bytes 12582912 | tf_op jit(solution)/shard_map/convert_element_type | solution.py:72
  64.6 5.2 %constant_dynamic-slice_fusion.1 = (bf16[1,6,256,512]{3,2,1,0:T(8,128)(2,1)S(1)}, bf16[6,256,512]{2,1,0:T(8,128)(2,1)}, bf16[6,256,512]{2,1,0:T(8,128)(2,1)}, bf16[6,256,512]{2,1,0:T(8,128)(2,1)}) fusion(bf16[4,6,256,512]{3,2,1,0:T(8,128)(2,1)} %bitcast.43, s32[]{:T(128)S(6)} %select_n.255, s32[]{:T(128)S(6)} %select_n.261, s32[]{:T(128)S(6)} %select_n.259, ...), kind=kLoop, calls=%fused_computation.82 | loop fusion | bytes 12582928 | tf_op jit(solution)/shard_map/dynamic_slice | solution.py:75
  69.8 4.3 collective-permute-start.2
  74.1 0.9 collective-permute-start
  75.1 0.7 gather_fusion.4
  75.8 0.7 gather_fusion.3
  77.1 0.6 gather_fusion
  77.7 131.7 %collective-permute-done.2 = bf16[6,256,512]{2,1,0:T(8,128)(2,1)} collective-permute-done((bf16[6,256,512]{2,1,0:T(8,128)(2,1)}, bf16[6,256,512]{2,1,0:T(8,128)(2,1)}, u32[]{:S(2)}, u32[]{:S(2)}) %collective-permute-start.2) | collective-permute-done | bytes 1572896 | tf_op jit(solution)/shard_map/ppermute | solution.py:78
  209.4 143.1 %collective-permute-done.1 = bf16[6,256,512]{2,1,0:T(8,128)(2,1)} collective-permute-done((bf16[6,256,512]{2,1,0:T(8,128)(2,1)}, bf16[6,256,512]{2,1,0:T(8,128)(2,1)}, u32[]{:S(2)}, u32[]{:S(2)}) %collective-permute-start.1) | collective-permute-done | bytes 1572896 | tf_op jit(solution)/shard_map/ppermute | solution.py:78
  352.5 5.8 %pad_maximum_fusion = bf16[4,6,256,512]{3,2,1,0:T(8,128)(2,1)} fusion(bf16[1,6,256,512]{3,2,1,0:T(8,128)(2,1)} %bitcast.7, bf16[1,6,256,512]{3,2,1,0:T(8,128)(2,1)} %bitcast.5, bf16[1,6,256,512]{3,2,1,0:T(8,128)(2,1)} %bitcast.3, bf16[1,6,256,512]{3,2,1,0:T(8,128)(2,1)S(1)} %get-tuple-element.13), kind=kLoop, calls=%fused_computation.13 | loop fusion | flops 9437184 | bytes 12582912 | tf_op jit(solution)/shard_map/stack | solution.py:79
  358.3 6.3 %gather_fusion.2 = bf16[4,6,256,512]{3,2,1,0:T(8,128)(2,1)} fusion(bf16[4,6,256,512]{3,2,1,0:T(8,128)(2,1)} %pad_maximum_fusion, s32[1024]{0:T(1024)S(1)} %pad_clamp_fusion.5), kind=kCustom, calls=%fused_computation.2 | custom fusion | bytes 12582928 | tf_op jit(solution)/shard_map/gather | solution.py:79
  364.6 6.8 %gather_fusion.5 = bf16[18,256,512]{2,1,0:T(8,128)(2,1)} fusion(bf16[24,256,512]{2,1,0:T(8,128)(2,1)} %bitcast.45, s32[1024]{0:T(1024)S(1)} %pad_clamp_fusion.3), kind=kCustom, calls=%fused_computation.5 | custom fusion | bytes 9437256 | tf_op jit(solution)/shard_map/gather | solution.py:85
  371.3 3.4 fusion
  374.7 1.6 copy.42
  376.4 0.8 sort.35
  377.4 0.7 gather_fusion.8
  378.5 8.0 %gather_fusion.9 = bf16[24,256,512]{2,1,0:T(8,128)(2,1)} fusion(bf16[28,256,512]{2,1,0:T(8,128)(2,1)} %all-to-all-done, s32[1024]{0:T(1024)S(1)} %pad_clamp_fusion), kind=kCustom, calls=%fused_computation.9 | custom fusion | bytes 12583008 | tf_op jit(solution)/shard_map/gather | solution.py:55
  386.5 33.2 %all-gather.2.cloned.1.call-done = bf16[6,512,512]{1,2,0:T(8,128)(2,1)} async-done(((bf16[6,256,512]{1,2,0:T(8,128)(2,1)}), bf16[6,512,512]{1,2,0:T(8,128)(2,1)}) %all-gather.2.cloned.1.call-update) | async-done | bytes 3145744 | tf_op jit(solution)/shard_map/all_gather | solution.py:91
  419.6 10.0 %convert_bitcast_fusion = bf16[4,6,256,512]{2,3,0,1:T(8,128)(2,1)} fusion(bf16[4,6,256,512]{3,2,1,0:T(8,128)(2,1)} %bitcast.47, bf16[6,512,512]{1,2,0:T(8,128)(2,1)} %all-gather.2.cloned.1.call-done), kind=kOutput, calls=%fused_computation.16 | convolution fusion | flops 3224371200 | bytes 15728640 | tf_op jit(solution)/shard_map/olrd,lde->olre/dot_general | solution.py:88
  429.6 8.6 %copy.50 = bf16[4,6,256,512]{3,2,1,0:T(8,128)(2,1)} copy(bf16[4,6,256,512]{2,3,0,1:T(8,128)(2,1)} %convert_bitcast_fusion) | data formatting | bytes 12582912 | tf_op jit(solution)/shard_map/convert_element_type | solution.py:94
  (63 shorter events, 2.6 us)
Async XLA Ops:
  6.5 7.6 %copy-start = (bf16[4,512,512]{2,1,0:T(8,128)(2,1)S(1)}, bf16[4,512,512]{2,1,0:T(8,128)(2,1)}, u32[]{:S(2)}) copy-start(bf16[4,512,512]{2,1,0:T(8,128)(2,1)} %param.8) | copy-start | bytes 6291460
  49.8 6.5 %copy-start.3 = (s32[24,3]{0,1:T(4,128)S(1)}, s32[24,3]{0,1:T(4,128)}, u32[]{:S(2)}) copy-start(s32[24,3]{0,1:T(4,128)} %param.12) | copy-start | bytes 868
  49.8 7.8 %copy-start.2 = (bf16[6,256,512]{2,1,0:T(8,128)(2,1)S(1)}, bf16[6,256,512]{2,1,0:T(8,128)(2,1)}, u32[]{:S(2)}) copy-start(bf16[6,256,512]{2,1,0:T(8,128)(2,1)} %param.11) | copy-start | bytes 4718596
  49.8 328.7 %all-to-all-start = ((bf16[28,256,512]{2,1,0:T(8,128)(2,1)}), bf16[28,256,512]{2,1,0:T(8,128)(2,1)}, u32[]{:S(2)}, u32[]{:S(2)}) async-start(bf16[28,256,512]{2,1,0:T(8,128)(2,1)} %scatter_fusion), calls=%async_computation | async-start | bytes 14680064 | tf_op jit(solution)/shard_map/all_to_all | solution.py:52
  56.3 363.4 %all-gather.2.cloned.1.call-start = ((), (), s32[]{:S(2)}) async-start(), calls=%async_computation.1 | async-start | bytes 4718592 | tf_op jit(solution)/shard_map/all_gather | solution.py:91
  69.8 7.1 %copy-start.4 = (f32[24,3]{0,1:T(4,128)S(1)}, f32[24,3]{0,1:T(4,128)}, u32[]{:S(2)}) copy-start(f32[24,3]{0,1:T(4,128)} %param.13) | copy-start | bytes 868
  69.8 139.6 %collective-permute-start.2 = (bf16[6,256,512]{2,1,0:T(8,128)(2,1)}, bf16[6,256,512]{2,1,0:T(8,128)(2,1)}, u32[]{:S(2)}, u32[]{:S(2)}) collective-permute-start(bf16[6,256,512]{2,1,0:T(8,128)(2,1)} %get-tuple-element.14), channel_id=1, source_target_pairs={{0,12},{4,0},{8,4},{12,8},{1,13},{5,1},{9,5},{13,9},{2,14},{6,2},{... | collective-permute-start | bytes 4718600 | tf_op jit(solution)/shard_map/ppermute | solution.py:78
  74.1 278.4 %collective-permute-start.1 = (bf16[6,256,512]{2,1,0:T(8,128)(2,1)}, bf16[6,256,512]{2,1,0:T(8,128)(2,1)}, u32[]{:S(2)}, u32[]{:S(2)}) collective-permute-start(bf16[6,256,512]{2,1,0:T(8,128)(2,1)} %get-tuple-element.15), channel_id=1, source_target_pairs={{0,8},{4,12},{8,0},{12,4},{1,9},{5,13},{9,1},{13,5},{2,10},{6,14},... | collective-permute-start | bytes 4718600 | tf_op jit(solution)/shard_map/ppermute | solution.py:78
  74.1 278.4 %collective-permute-start = (bf16[6,256,512]{2,1,0:T(8,128)(2,1)}, bf16[6,256,512]{2,1,0:T(8,128)(2,1)}, u32[]{:S(2)}, u32[]{:S(2)}) collective-permute-start(bf16[6,256,512]{2,1,0:T(8,128)(2,1)} %get-tuple-element.16), channel_id=1, source_target_pairs={{0,4},{4,8},{8,12},{12,0},{1,5},{5,9},{9,13},{13,1},{2,6},{6,10},{... | collective-permute-start | bytes 4718600 | tf_op jit(solution)/shard_map/ppermute | solution.py:78
  419.6 18.6 %copy-start.1 = (bf16[4,512,512]{2,1,0:T(8,128)(2,1)S(1)}, bf16[4,512,512]{2,1,0:T(8,128)(2,1)}, u32[]{:S(2)}) copy-start(bf16[4,512,512]{2,1,0:T(8,128)(2,1)} %param.8) | copy-start | bytes 6291460
Sparse Core Ops, SparseCore 0:
  376.4 43.1 all-gather.1
